TPU v7x, 32 devices: a whole 2x2x4 slice. The times are simulated.
32 devices in a mesh: chain: 2 (over x), slab: 16 (over z, y, core).
Axes of the slice: x: 2, y: 2, z: 4, core: 2. Of those that a mesh axis runs over, the one named last changes fastest.
Arguments:
- whitened: float32 [1024, 256, 256], P(('chain', 'slab')), parts along dimension 0, may hold values from -6 to 6
- counts: int32 [1024, 256, 256], P(('chain', 'slab')), parts along dimension 0, may hold values from 0 to 24
- exposure: int32 [1024, 256, 256], P(('chain', 'slab')), parts along dimension 0, may hold values from 1 to 12
- cholesky_east: float32 [512, 512], replicated, as said below
- cholesky_north: float32 [256, 256], replicated, as said below
- cholesky_time: float32 [256, 256], replicated, as said below
Outputs:
- gradient: float32 [1024, 256, 256], P(('chain', 'slab')), parts along dimension 0
- density: float32 [2], P('chain'), parts along dimension 0
There are 2 independent parts, one for each index of `chain`. A program takes and returns all parts, laid end to end along the dimension named above; an argument that names none is the same for every part. Nothing has to cross between parts.
Inputs may be any that keep to these rules, and one draw needn't show every extreme that they name: `cholesky_east`: lower triangular with a positive diagonal, each row of unit length. `cholesky_north`: lower triangular with a positive diagonal, each row of unit length. `cholesky_time`: lower triangular with a positive diagonal, each row of unit length.
All inputs are finite; a program needn't handle non-finite values.
Results may differ from a plain program's by a relative error of at most 0.00008.
Values sent between devices are 32-bit elements; how exact they have to be, the bound alone decides.
A program may use at most 128 MiB of HBM per device.

v0:
```python
import functools

import jax
import jax.numpy as jnp
from jax import lax
from jax.experimental import pallas as pl
from jax.experimental.pallas import tpu as pltpu
from jax.sharding import PartitionSpec as P

field_scale = 0.6
QUARTERS = 4
LANES = 128
AHEAD = 12
DEPTH = 16
FORWARD_LAG = (1, 1, 2, 3)
BACKWARD_LAG = (7, 6, 5, 4)
VMEM_BYTES = 67043328


def split(values):
    high = values.astype(jnp.bfloat16)
    low = (values - high.astype(jnp.float32)).astype(jnp.bfloat16)
    return high, low


def hhl(matrix, axis):
    high, low = split(matrix)
    return jnp.concatenate([high, high, low], axis=axis)


def hlh(matrix, axis):
    high, low = split(matrix)
    return jnp.concatenate([high, low, high], axis=axis)


def dot(left, right):
    return jnp.dot(left, right, preferred_element_type=jnp.float32)


def kernel(
    group, parts, q_hbm, cnt_hbm, exp_hbm, east, prior, out_hbm, density,
    own, f0, f1, cnt, wgt, b0, b1, res, spare, out, fwd, bwd, acc, near, far,
    send_in, recv_p, recv_c, recv_e, send_z, recv_f0, recv_f1, recv_b0, recv_b1,
    send_r, send_s, send_g, keep_g, recv_g,
    send_near, recv_near, send_far, recv_far,
):
    slab = lax.axis_index("slab")
    quarter = slab // group
    place = slab % group
    chunks = own.shape[0]
    rows = own.shape[1]
    planes = q_hbm.shape[0]
    lines = q_hbm.shape[1] // group
    depth = res.shape[0]
    lanes = own.shape[2]

    def device(quarter_of, place_of):
        return {"slab": quarter_of * group + place_of}

    barrier = pltpu.get_barrier_semaphore()
    for j in range(1, group):
        pl.semaphore_signal(barrier, inc=1, device_id=device(quarter, lax.rem(place + j, group)), device_id_type=pl.DeviceIdType.MESH)
    for j in range(1, QUARTERS):
        pl.semaphore_signal(barrier, inc=1, device_id=device(lax.rem(quarter + j, QUARTERS), place), device_id_type=pl.DeviceIdType.MESH)
    pl.semaphore_wait(barrier, group + QUARTERS - 2)

    def remote(src, dst, send_sem, recv_sem, target):
        pltpu.make_async_remote_copy(
            src_ref=src, dst_ref=dst, send_sem=send_sem, recv_sem=recv_sem,
            device_id=target, device_id_type=pl.DeviceIdType.MESH,
        ).start()

    def await_bytes(ref, sem):
        pltpu.make_async_copy(ref, ref, sem).wait()

    def times_of(chunk):
        return pl.ds(pl.multiple_of(lax.rem(chunk, parts) * lanes, lanes), lanes)

    def spread(chunk):
        mine = pl.ds(place * planes, planes)
        line = chunk // parts
        for k, (src, dst, recv) in enumerate(((q_hbm, own, recv_p), (cnt_hbm, cnt, recv_c), (exp_hbm, wgt, recv_e))):
            for j in range(1, group):
                to = lax.rem(place + j, group)
                remote(
                    src.at[:, to * lines + line, times_of(chunk)], dst.at[chunk, mine],
                    send_in.at[k], recv.at[chunk], device(quarter, to),
                )
            pltpu.make_async_copy(
                src.at[:, place * lines + line, times_of(chunk)], dst.at[chunk, mine], recv.at[chunk]
            ).start()

    def collect(chunk, slot):
        there = (slice(None), place * lines + chunk // parts, times_of(chunk))
        for j in range(1, group):
            to = lax.rem(place + j, group)
            remote(out.at[slot, pl.ds(to * planes, planes)], out_hbm.at[there], send_g.at[slot], recv_g, device(quarter, to))
        pltpu.make_async_copy(out.at[slot, pl.ds(place * planes, planes)], out_hbm.at[there], keep_g.at[slot]).start()

    def await_collected(slot):
        if group > 1:
            await_bytes(out.at[slot, pl.ds(0, (group - 1) * planes)], send_g.at[slot])
        await_bytes(out.at[slot, pl.ds(0, planes)], keep_g.at[slot])

    def onward(q, chunk):
        await_bytes(own.at[chunk], recv_p.at[chunk])
        if q == 0:
            remote(own.at[chunk], f1.at[chunk], send_z.at[1], recv_f1.at[chunk], device(2, place))
            remote(own.at[chunk], f0.at[chunk], send_z.at[0], recv_f0.at[chunk], device(1, place))
        if q == 1:
            remote(own.at[chunk], f0.at[chunk], send_z.at[0], recv_f0.at[chunk], device(2, place))

    def forward(q, chunk):
        slot = lax.rem(chunk, depth)
        await_bytes(cnt.at[chunk], recv_c.at[chunk])
        await_bytes(wgt.at[chunk], recv_e.at[chunk])
        if q >= 1:
            await_bytes(f0.at[chunk], recv_f0.at[chunk])
        if q == 2:
            await_bytes(f1.at[chunk], recv_f1.at[chunk])

        @pl.when(chunk >= depth)
        def _():
            for _ in range((0, 0, 1, 2)[q]):
                await_bytes(res.at[slot], send_r.at[slot])
            if q == 2:
                await_bytes(spare.at[slot], send_s.at[slot])

        terms = ((own,), (f0, own), (f1, f0, own), (own,))[q]
        high_low = hlh(jnp.concatenate([ref[chunk] for ref in terms], axis=0), 0)
        count = 2 if q == 2 else 1
        field = dot(fwd[0 : count * rows, 0 : 3 * len(terms) * rows], high_low)
        if q == 2:
            spare[slot] = field[rows:]
            field = field[:rows]
        if q == 3:
            field = field + f0[chunk]
        log_rate = field_scale * field
        observed = cnt[chunk].astype(jnp.float32)
        intensity = wgt[chunk].astype(jnp.float32) * jnp.exp(log_rate)
        acc[...] += observed * log_rate - intensity
        res[slot] = observed - intensity
        if q == 2:
            remote(spare.at[slot], f0.at[chunk], send_s.at[slot], recv_f0.at[chunk], device(3, place))
            remote(res.at[slot], b0.at[chunk], send_r.at[slot], recv_b0.at[chunk], device(1, place))
        if q == 3:
            remote(res.at[slot], b1.at[chunk], send_r.at[slot], recv_b1.at[chunk], device(1, place))
            remote(res.at[slot], b0.at[chunk], send_r.at[slot], recv_b0.at[chunk], device(2, place))

    def backward(q, chunk):
        slot = lax.rem(chunk, depth)
        if q <= 2:
            await_bytes(b0.at[chunk], recv_b0.at[chunk])
        if q == 1:
            await_bytes(b1.at[chunk], recv_b1.at[chunk])

        @pl.when(chunk >= depth)
        def _():
            await_collected(slot)
            if q == 1:
                await_bytes(spare.at[slot], send_s.at[slot])

        terms = [res[slot]]
        if q in (1, 2):
            terms.append(b0[chunk])
        if q == 1:
            terms.append(b1[chunk])
        high_low = hlh(jnp.concatenate(terms, axis=0), 0)
        count = 2 if q == 1 else 1
        value = dot(bwd[0 : count * rows, 0 : 3 * len(terms) * rows], high_low)
        if q == 1:
            spare[slot] = value[rows:]
            remote(spare.at[slot], b0.at[chunk], send_s.at[slot], recv_b0.at[chunk], device(0, place))
            value = value[:rows]
        if q == 0:
            value = value + b0[chunk]
        out[slot] = value
        collect(chunk, slot)

    def block(r0, r1, c0, c1):
        return east[r0 * rows : r1 * rows, c0 * rows : c1 * rows]

    def factors(q):
        left = (block(0, 1, 0, 1), block(1, 2, 0, 2), block(2, 4, 0, 3), block(3, 4, 3, 4))[q]
        fwd[0 : left.shape[0], 0 : 3 * left.shape[1]] = hhl(left, 1)
        if q == 1:
            back = jnp.concatenate([block(1, 4, 1, 2).T, block(1, 4, 0, 1).T], axis=0)
        else:
            back = (block(0, 1, 0, 1), None, block(2, 4, 2, 3), block(3, 4, 3, 4))[q].T
        bwd[0 : back.shape[0], 0 : 3 * back.shape[1]] = hhl(back, 1)

    def fold(tile):
        return sum(tile[:, k * lanes : (k + 1) * lanes] for k in range(tile.shape[1] // lanes))

    def send_sum_near():
        cells = jnp.sum(acc[...].reshape(rows // 8, 8, lanes), axis=0)
        near[place] = cells - 0.5 * fold(prior[...])
        for j in range(1, group):
            remote(near.at[place], near.at[place], send_near, recv_near, device(quarter, lax.rem(place + j, group)))

    def send_sum_far():
        if group > 1:
            others = near.at[pl.ds(0, group - 1)]
            await_bytes(others, send_near)
            await_bytes(others, recv_near)
        far[quarter] = jnp.sum(near[...], axis=0)
        for j in range(1, QUARTERS):
            remote(far.at[quarter], far.at[quarter], send_far, recv_far, device(lax.rem(quarter + j, QUARTERS), place))

    ahead = min(AHEAD, chunks)

    def start(chunk, carry):
        spread(chunk)
        return carry

    lax.fori_loop(0, ahead, start, 0)
    acc[...] = jnp.zeros_like(acc)
    for q in range(QUARTERS):
        @pl.when(quarter == q)
        def _(q=q):
            factors(q)

    last = chunks + max(FORWARD_LAG)

    def turn(i, carry):
        @pl.when(i + ahead < chunks)
        def _():
            spread(i + ahead)

        for q in range(QUARTERS):
            @pl.when((quarter == q) & (i < chunks))
            def _(q=q):
                onward(q, i)

            @pl.when((quarter == q) & (i >= FORWARD_LAG[q]) & (i < chunks + FORWARD_LAG[q]))
            def _(q=q):
                forward(q, i - FORWARD_LAG[q])

            @pl.when((quarter == q) & (i >= BACKWARD_LAG[q]) & (i < chunks + BACKWARD_LAG[q]))
            def _(q=q):
                backward(q, i - BACKWARD_LAG[q])

        @pl.when(i == last - 1)
        def _():
            send_sum_near()

        @pl.when(i == last + 1)
        def _():
            send_sum_far()

        return carry

    lax.fori_loop(0, chunks + max(BACKWARD_LAG), turn, 0)

    others = far.at[pl.ds(0, QUARTERS - 1)]
    await_bytes(others, send_far)
    await_bytes(others, recv_far)
    density[...] = jnp.sum(far[...], axis=0)

    away = (slice(None), pl.ds(0, (group - 1) * lines))
    if group > 1:
        for k, src in enumerate((q_hbm, cnt_hbm, exp_hbm)):
            await_bytes(src.at[away], send_in.at[k])
    for slot in range(depth):
        await_collected(slot)

    @pl.when(quarter == 0)
    def _():
        await_bytes(own, send_z.at[1])

    @pl.when(quarter <= 1)
    def _():
        await_bytes(own, send_z.at[0])

    @pl.when(quarter >= 2)
    def _():
        for slot in range(depth):
            await_bytes(res.at[slot], send_r.at[slot])

    @pl.when(quarter == 3)
    def _():
        for slot in range(depth):
            await_bytes(res.at[slot], send_r.at[slot])

    @pl.when((quarter == 1) | (quarter == 2))
    def _():
        for slot in range(depth):
            await_bytes(spare.at[slot], send_s.at[slot])

    if group > 1:
        await_bytes(out_hbm.at[away], recv_g)


def exchange(partly, counts, exposure, east, prior, group):
    planes, all_lines, times = partly.shape
    rows = planes * group
    parts = times // LANES
    chunks = all_lines // group * parts
    depth = min(DEPTH, chunks)
    whole = lambda kind: pltpu.VMEM((chunks, rows, LANES), kind)
    ring = lambda: pltpu.VMEM((depth, rows, LANES), jnp.float32)
    stacked = lambda: pltpu.VMEM((2 * rows, 9 * rows), jnp.bfloat16)
    any_space = pl.BlockSpec(memory_space=pl.ANY)
    in_vmem = pl.BlockSpec(memory_space=pltpu.VMEM)
    dma = pltpu.SemaphoreType.DMA
    return pl.pallas_call(
        functools.partial(kernel, group, parts),
        out_shape=(
            jax.ShapeDtypeStruct(partly.shape, jnp.float32),
            jax.ShapeDtypeStruct((8, LANES), jnp.float32),
        ),
        in_specs=[any_space] * 3 + [in_vmem] * 2,
        out_specs=(any_space, in_vmem),
        scratch_shapes=[whole(jnp.float32) for _ in range(3)]
        + [whole(jnp.int32) for _ in range(2)]
        + [whole(jnp.float32) for _ in range(2)]
        + [ring() for _ in range(3)]
        + [stacked() for _ in range(2)]
        + [
            pltpu.VMEM((rows, LANES), jnp.float32),
            pltpu.VMEM((group, 8, LANES), jnp.float32),
            pltpu.VMEM((QUARTERS, 8, LANES), jnp.float32),
        ]
        + [dma((3,))]
        + [dma((chunks,)) for _ in range(3)]
        + [dma((2,))]
        + [dma((chunks,)) for _ in range(4)]
        + [dma((depth,)) for _ in range(4)]
        + [dma] * 5,
        compiler_params=pltpu.CompilerParams(
            collective_id=0, has_side_effects=True, vmem_limit_bytes=VMEM_BYTES
        ),
    )(partly, counts, exposure, east, prior)


def prepare_kernel(w_ref, north, time, q_ref, squares, left, right):
    @pl.when(pl.program_id(0) == 0)
    def _():
        left[...] = hhl(north[...], 1)
        right[...] = hhl(time[...].T, 0)
        squares[...] = jnp.zeros_like(squares)

    block, lines, times = w_ref.shape
    values = w_ref[...].reshape(block * lines, times)
    squares[...] += jnp.sum((values * values).reshape(-1, 8, times), axis=0)
    partly = dot(hlh(values, 1), right[...])
    for a in range(block):
        q_ref[a] = dot(left[...], hlh(partly[a * lines : (a + 1) * lines], 0))


def finish_kernel(scale, g_ref, w_ref, north, time, terms, out_ref, density, left, right):
    @pl.when(pl.program_id(0) == 0)
    def _():
        left[...] = hhl(north[...].T, 1)
        right[...] = hhl(time[...], 0)
        density[0] = jnp.sum(terms[...]) * scale

    block, lines, times = g_ref.shape
    values = g_ref[...].reshape(block * lines, times)
    partly = dot(hlh(values, 1), right[...])
    for a in range(block):
        adjoint = dot(left[...], hlh(partly[a * lines : (a + 1) * lines], 0))
        out_ref[a] = field_scale * adjoint - w_ref[a]


BLOCK = 2


def planes_spec(lines, times):
    return pl.BlockSpec((BLOCK, lines, times), lambda i: (i, 0, 0))


def fixed_spec(*shape):
    return pl.BlockSpec(shape, lambda i: (0, 0))


def stacked_pair(lines, times):
    return [pltpu.VMEM((lines, 3 * lines), jnp.bfloat16), pltpu.VMEM((3 * times, times), jnp.bfloat16)]


def prepare(whitened, north, time):
    planes, lines, times = whitened.shape
    return pl.pallas_call(
        prepare_kernel,
        grid=(planes // BLOCK,),
        out_shape=[jax.ShapeDtypeStruct(whitened.shape, jnp.float32), jax.ShapeDtypeStruct((8, times), jnp.float32)],
        in_specs=[planes_spec(lines, times), fixed_spec(lines, lines), fixed_spec(times, times)],
        out_specs=[planes_spec(lines, times), fixed_spec(8, times)],
        scratch_shapes=stacked_pair(lines, times),
    )(whitened, north, time)


def finish(adjoint, whitened, north, time, terms, scale):
    planes, lines, times = whitened.shape
    return pl.pallas_call(
        functools.partial(finish_kernel, scale),
        grid=(planes // BLOCK,),
        out_shape=[jax.ShapeDtypeStruct(whitened.shape, jnp.float32), jax.ShapeDtypeStruct((1,), jnp.float32)],
        in_specs=[planes_spec(lines, times)] * 2
        + [fixed_spec(lines, lines), fixed_spec(times, times), fixed_spec(*terms.shape)],
        out_specs=[planes_spec(lines, times), pl.BlockSpec(memory_space=pltpu.SMEM)],
        scratch_shapes=stacked_pair(lines, times),
    )(adjoint, whitened, north, time, terms)


def per_device(whitened, counts, exposure, cholesky_east, cholesky_north, cholesky_time):
    slabs = lax.axis_size("slab")
    cell_count = whitened.shape[0] * whitened.shape[1] * whitened.shape[2] * slabs
    partly, squares = prepare(whitened, cholesky_north, cholesky_time)
    adjoint, terms = exchange(partly, counts, exposure, cholesky_east, squares, slabs // QUARTERS)
    gradient, density = finish(adjoint, whitened, cholesky_north, cholesky_time, terms, 1.0 / cell_count)
    return (gradient, density)


def solution(mesh):
    placed = (
        P(("chain", "slab"), None, None),
        P(("chain", "slab"), None, None),
        P(("chain", "slab"), None, None),
        P(),
        P(),
        P(),
    )
    return jax.shard_map(
        per_device,
        mesh=mesh,
        in_specs=placed,
        out_specs=(P(("chain", "slab"), None, None), P("chain")),
        check_vma=False,
    )
```

profile of v0, /device:TPU:0, one launch (start us, length us, event | category | flops | bytes accessed | tf_op | source)
XLA Modules:
  0.0 471.6 jit_solution(878511859862339492)
XLA Ops:
  0.6 20.2 %shard_map.77 = (f32[32,256,256]{2,1,0:T(8,128)}, f32[8,256]{1,0:T(8,128)}) custom-call(f32[32,256,256]{2,1,0:T(8,128)} %w_ref.3, f32[256,256]{1,0:T(8,128)} %north.3, f32[256,256]{1,0:T(8,128)} %time.3), custom_call_target="tpu_custom_call" | custom-call | tf_op jit(solution)/shard_map/pallas_call | solution.py:383
  20.8 429.0 %shard_map.78 = (f32[32,256,256]{2,1,0:T(8,128)}, f32[8,128]{1,0:T(8,128)}) custom-call(f32[32,256,256]{2,1,0:T(8,128)} %get-tuple-element.6.q_hbm, s32[32,256,256]{2,1,0:T(8,128)} %cnt_hbm.1, s32[32,256,256]{2,1,0:T(8,128)} %exp_hbm.1, f32[512,512]{1,0:T(8,128)} %east.1, f32[8,256]{1,0:T(8,128)} %get-tuple-element.7.prior), custom_call_target="tpu_custom_call" | custom-call | tf_op jit(solution)/shard_map/pallas_call | solution.py:306
  449.8 21.8 %shard_map.79 = (f32[32,256,256]{2,1,0:T(8,128)}, f32[1]{0:T(128)}) custom-call(f32[32,256,256]{2,1,0:T(8,128)} %get-tuple-element.8.g_ref, f32[32,256,256]{2,1,0:T(8,128)} %w_ref.3, f32[256,256]{1,0:T(8,128)} %north.3, f32[256,256]{1,0:T(8,128)} %time.3, f32[8,128]{1,0:T(8,128)} %get-tuple-element.9.terms), custom_call_target="tpu_custom_call" | custom-call | tf_op jit(solution)/shard_map/pallas_call | solution.py:395
where the time goes:
time: 473 us; the launch traced here: 472 us
  Pallas kernels  471 us (100%)
    pallas_call x1, Pallas kernels, exchange(): pl.pallas_call(functools.partial(kernel, group, parts), out_shape=(jax.Sh...  429 us
    pallas_call x1, Pallas kernels, finish(): pl.pallas_call(functools.partial(finish_kernel, scale), grid=(planes // B...  21.8 us
    pallas_call x1, Pallas kernels, prepare(): pl.pallas_call(prepare_kernel, grid=(planes // BLOCK,), out_shape=[jax.Sh...  20.2 us

commit v1 on v0

v1 whole, which is shorter than its diff:
```python
import functools

import jax
import jax.numpy as jnp
from jax import lax
from jax.experimental import pallas as pl
from jax.experimental.pallas import tpu as pltpu
from jax.sharding import PartitionSpec as P

field_scale = 0.6
QUARTERS = 4
LANES = 128
AHEAD = 4
RING = 16
BANDS = 4
SENT = 4
FORWARD_LAG = (2, 4, 0, 0)
BACKWARD_LAG = (10, 8, 4, 1)
VMEM_BYTES = 67043328


def split(values):
    high = values.astype(jnp.bfloat16)
    low = (values - high.astype(jnp.float32)).astype(jnp.bfloat16)
    return high, low


def hhl(matrix, axis):
    high, low = split(matrix)
    return jnp.concatenate([high, high, low], axis=axis)


def hlh(matrix, axis):
    high, low = split(matrix)
    return jnp.concatenate([high, low, high], axis=axis)


def dot(left, right):
    return jnp.dot(left, right, preferred_element_type=jnp.float32)


def kernel(
    group, parts, w_hbm, cnt_hbm, exp_hbm, east, north, time, out_hbm, density,
    held, q_own, squares, left, onto, back, pending, own, f0, f1, cnt, wgt, b0, b1, res, spare, out, fwd, bwd, acc, near, far,
    send_in, recv_p, recv_o, recv_f, recv_b, send_z, send_r, send_g, keep_g, recv_g,
    send_near, recv_near, send_far, recv_far, load_first, load_rest,
):
    slab = lax.axis_index("slab")
    quarter = slab // group
    place = slab % group
    ring = own.shape[0]
    rows = own.shape[1]
    lanes = own.shape[2]
    planes, north_cells, times = held.shape
    lines = north_cells // group
    chunks = lines * parts
    rings = out.shape[0]
    band = north_cells // BANDS
    per_band = band // group * parts

    first = (slice(None), pl.ds(0, band))
    rest = (slice(None), pl.ds(band, north_cells - band))
    pltpu.make_async_copy(w_hbm.at[first], held.at[first], load_first).start()
    pltpu.make_async_copy(w_hbm.at[rest], held.at[rest], load_rest).start()

    def device(quarter_of, place_of):
        return {"slab": quarter_of * group + place_of}

    barrier = pltpu.get_barrier_semaphore()
    for j in range(1, group):
        pl.semaphore_signal(barrier, inc=1, device_id=device(quarter, lax.rem(place + j, group)), device_id_type=pl.DeviceIdType.MESH)
    for j in range(1, QUARTERS):
        pl.semaphore_signal(barrier, inc=1, device_id=device(lax.rem(quarter + j, QUARTERS), place), device_id_type=pl.DeviceIdType.MESH)
    left[...] = hhl(north[...], 1)
    onto[...] = hhl(time[...].T, 0)
    back[...] = hhl(time[...], 0)
    acc[...] = jnp.zeros_like(acc)
    squares[...] = jnp.zeros_like(squares)
    pl.semaphore_wait(barrier, group + QUARTERS - 2)

    def remote(src, dst, send_sem, recv_sem, target):
        pltpu.make_async_remote_copy(
            src_ref=src, dst_ref=dst, send_sem=send_sem, recv_sem=recv_sem,
            device_id=target, device_id_type=pl.DeviceIdType.MESH,
        ).start()

    def await_bytes(ref, sem):
        pltpu.make_async_copy(ref, ref, sem).wait()

    def await_slots(count, sem):
        if count:
            await_bytes(own.at[pl.ds(0, count)], sem)

    def slot_of(chunk):
        return lax.rem(chunk, ring)

    def line_of(chunk, place_of):
        return chunk // parts * group + place_of

    def times_of(chunk):
        return pl.ds(pl.multiple_of(lax.rem(chunk, parts) * lanes, lanes), lanes)

    def spread(chunk, arrays):
        mine = pl.ds(place * planes, planes)
        slot = slot_of(chunk)
        for k in arrays:
            src, dst, recv = ((q_own, own, recv_p), (cnt_hbm, cnt, recv_o), (exp_hbm, wgt, recv_o))[k]
            for j in range(1, group):
                to = lax.rem(place + j, group)
                remote(
                    src.at[:, line_of(chunk, to), times_of(chunk)], dst.at[slot, mine],
                    send_in.at[k], recv.at[slot], device(quarter, to),
                )
            pltpu.make_async_copy(
                src.at[:, line_of(chunk, place), times_of(chunk)], dst.at[slot, mine], recv.at[slot]
            ).start()

    def square(cells):
        squares[...] += jnp.sum((cells * cells).reshape(-1, 8, times), axis=0)

    def begin():
        few = min(planes, 4)

        def some(i, carry):
            mixed = []
            for k in range(few):
                cells = held[i * few + k, 0:band]
                square(cells)
                mixed.append(dot(hhl(north[0:band, 0:band], 1), hlh(cells, 0)))
            partly = dot(hlh(jnp.concatenate(mixed, axis=0), 1), onto[...])
            for k in range(few):
                q_own[i * few + k, 0:band] = partly[k * band : (k + 1) * band]
            return carry

        lax.fori_loop(0, planes // few, some, 0)

    def proceed(step):
        part = planes // per_band
        rows_of = pl.ds(pl.multiple_of((step // per_band + 1) * band, band), band)
        for k in range(part):
            plane = lax.rem(step, per_band) * part + k
            square(held[plane, rows_of])
            mixed = dot(left[rows_of], hlh(held[plane], 0))
            q_own[plane, rows_of] = dot(hlh(mixed, 1), onto[...])

    def collect(line, slot):
        there = (slice(None), line * group + place)
        for j in range(1, group):
            to = lax.rem(place + j, group)
            remote(out.at[slot, pl.ds(to * planes, planes)], out_hbm.at[there], send_g.at[slot], recv_g, device(quarter, to))
        pltpu.make_async_copy(out.at[slot, pl.ds(place * planes, planes)], out_hbm.at[there], keep_g.at[slot]).start()

    def await_collected(line):
        slot = lax.rem(line, rings)
        if group > 1:
            await_bytes(out.at[slot, pl.ds(0, (group - 1) * planes)], send_g.at[slot])
        await_bytes(out.at[slot, pl.ds(0, planes)], keep_g.at[slot])

    def onward(q, chunk):
        slot = slot_of(chunk)
        await_bytes(own.at[slot], recv_p.at[slot])
        if q == 0:
            remote(own.at[slot], f1.at[slot], send_z.at[slot], recv_f.at[slot], device(2, place))
            remote(own.at[slot], f0.at[slot], send_z.at[slot], recv_f.at[slot], device(1, place))
        if q == 1:
            remote(own.at[slot], f0.at[slot], send_z.at[slot], recv_f.at[slot], device(2, place))

    def await_onward(q, chunk):
        slot = slot_of(chunk)
        await_slots((2, 1, 0, 0)[q], send_z.at[slot])

    def await_residual(q, chunk):
        slot = slot_of(chunk)
        await_slots((0, 0, 2, 2)[q], send_r.at[slot])

    def forward(q, chunk):
        slot = slot_of(chunk)
        await_slots(2, recv_o.at[slot])
        await_slots((0, 1, 2, 1)[q], recv_f.at[slot])

        @pl.when(chunk >= ring)
        def _():
            await_residual(q, chunk)

        terms = ((own,), (f0, own), (f1, f0, own), (own,))[q]
        high_low = hlh(jnp.concatenate([ref[slot] for ref in terms], axis=0), 0)
        count = 2 if q == 2 else 1
        field = dot(fwd[0 : count * rows, 0 : 3 * len(terms) * rows], high_low)
        if q == 2:
            spare[slot] = field[rows:]
            field = field[:rows]
        if q == 3:
            field = field + f0[slot]
        log_rate = field_scale * field
        observed = cnt[slot].astype(jnp.float32)
        intensity = wgt[slot].astype(jnp.float32) * jnp.exp(log_rate)
        acc[...] += observed * log_rate - intensity
        res[slot] = observed - intensity
        if q == 2:
            remote(spare.at[slot], f0.at[slot], send_r.at[slot], recv_f.at[slot], device(3, place))
            remote(res.at[slot], b0.at[slot], send_r.at[slot], recv_b.at[slot], device(1, place))
        if q == 3:
            remote(res.at[slot], b1.at[slot], send_r.at[slot], recv_b.at[slot], device(1, place))
            remote(res.at[slot], b0.at[slot], send_r.at[slot], recv_b.at[slot], device(2, place))

    def await_partial(q, chunk):
        slot = slot_of(chunk)
        if q == 1:
            await_bytes(spare.at[slot], send_r.at[slot])

    def backward(q, chunk):
        slot = slot_of(chunk)
        await_slots((1, 2, 1, 0)[q], recv_b.at[slot])

        @pl.when(chunk >= ring)
        def _():
            await_partial(q, chunk)

        terms = [res[slot]]
        if q in (1, 2):
            terms.append(b0[slot])
        if q == 1:
            terms.append(b1[slot])
        high_low = hlh(jnp.concatenate(terms, axis=0), 0)
        count = 2 if q == 1 else 1
        value = dot(bwd[0 : count * rows, 0 : 3 * len(terms) * rows], high_low)
        if q == 1:
            spare[slot] = value[rows:]
            remote(spare.at[slot], b0.at[slot], send_r.at[slot], recv_b.at[slot], device(0, place))
            value = value[:rows]
        if q == 0:
            value = value + b0[slot]
        pending[:, times_of(chunk)] = value

        @pl.when(lax.rem(chunk, parts) == parts - 1)
        def _():
            line = chunk // parts

            @pl.when(line >= rings)
            def _():
                await_collected(line)

            into = lax.rem(line, rings)
            out[into] = dot(hlh(pending[...], 1), back[...])
            collect(line, into)

    def block(r0, r1, c0, c1):
        return east[r0 * rows : r1 * rows, c0 * rows : c1 * rows]

    def factors(q):
        left = (block(0, 1, 0, 1), block(1, 2, 0, 2), block(2, 4, 0, 3), block(3, 4, 3, 4))[q]
        fwd[0 : left.shape[0], 0 : 3 * left.shape[1]] = hhl(left, 1)
        if q == 1:
            back = jnp.concatenate([block(1, 4, 1, 2).T, block(1, 4, 0, 1).T], axis=0)
        else:
            back = (block(0, 1, 0, 1), None, block(2, 4, 2, 3), block(3, 4, 3, 4))[q].T
        bwd[0 : back.shape[0], 0 : 3 * back.shape[1]] = hhl(back, 1)

    def fold(tile):
        return sum(tile[:, k * lanes : (k + 1) * lanes] for k in range(tile.shape[1] // lanes))

    def send_sum_near():
        cells = jnp.sum(acc[...].reshape(rows // 8, 8, lanes), axis=0)
        near[place] = cells - 0.5 * fold(squares[...])
        for j in range(1, group):
            remote(near.at[place], near.at[place], send_near, recv_near, device(quarter, lax.rem(place + j, group)))

    def send_sum_far():
        if group > 1:
            others = near.at[pl.ds(0, group - 1)]
            await_bytes(others, send_near)
            await_bytes(others, recv_near)
        far[quarter] = jnp.sum(near[...], axis=0)
        for j in range(1, QUARTERS):
            remote(far.at[quarter], far.at[quarter], send_far, recv_far, device(lax.rem(quarter + j, QUARTERS), place))

    ahead = min(AHEAD, chunks)

    def start(arrays):
        def body(chunk, carry):
            spread(chunk, arrays)
            return carry

        lax.fori_loop(0, ahead, body, 0)

    start((1, 2))
    await_bytes(held.at[first], load_first)
    begin()
    start((0,))
    await_bytes(held.at[rest], load_rest)
    last = chunks + max(FORWARD_LAG)

    for q in range(QUARTERS):
        @pl.when(quarter == q)
        def _(q=q):
            factors(q)

            def turn(i, carry):
                @pl.when(i + ahead < chunks)
                def _():
                    spread(i + ahead, (0, 1, 2))

                @pl.when((i >= SENT) & (i < chunks + SENT))
                def _():
                    await_onward(q, i - SENT)

                @pl.when(i < chunks)
                def _():
                    onward(q, i)

                @pl.when((i >= FORWARD_LAG[q]) & (i < chunks + FORWARD_LAG[q]))
                def _():
                    forward(q, i - FORWARD_LAG[q])

                @pl.when((i >= BACKWARD_LAG[q]) & (i < chunks + BACKWARD_LAG[q]))
                def _():
                    backward(q, i - BACKWARD_LAG[q])

                @pl.when(i == last - 1)
                def _():
                    send_sum_near()

                @pl.when(i == last + 1)
                def _():
                    send_sum_far()

                @pl.when(i < ahead)
                def _():
                    proceed(i)

                @pl.when(i + ahead < (BANDS - 1) * per_band)
                def _():
                    proceed(i + ahead)

                return carry

            lax.fori_loop(0, chunks + max(BACKWARD_LAG), turn, 0)

            def drain(chunk, carry):
                await_residual(q, chunk)
                await_partial(q, chunk)
                return carry

            lax.fori_loop(max(chunks - ring, 0), chunks, drain, 0)

    def collected(line, carry):
        await_collected(line)
        return carry

    lax.fori_loop(max(lines - rings, 0), lines, collected, 0)

    others = far.at[pl.ds(0, QUARTERS - 1)]
    await_bytes(others, send_far)
    await_bytes(others, recv_far)
    density[...] = jnp.sum(far[...], axis=0)

    away = (slice(None), pl.ds(0, (group - 1) * lines))
    if group > 1:
        for k, src in enumerate((q_own, cnt_hbm, exp_hbm)):
            await_bytes(src.at[away], send_in.at[k])
        await_bytes(out_hbm.at[away], recv_g)


def exchange(whitened, counts, exposure, east, north, time, group):
    planes, lines, times = whitened.shape
    rows = planes * group
    parts = times // LANES
    ring = lambda kind: pltpu.VMEM((RING, rows, LANES), kind)
    stacked = lambda: pltpu.VMEM((2 * rows, 9 * rows), jnp.bfloat16)
    any_space = pl.BlockSpec(memory_space=pl.ANY)
    in_vmem = pl.BlockSpec(memory_space=pltpu.VMEM)
    dma = pltpu.SemaphoreType.DMA
    return pl.pallas_call(
        functools.partial(kernel, group, parts),
        out_shape=(
            jax.ShapeDtypeStruct(whitened.shape, jnp.float32),
            jax.ShapeDtypeStruct((8, LANES), jnp.float32),
        ),
        in_specs=[any_space] * 3 + [in_vmem] * 3,
        out_specs=(any_space, in_vmem),
        scratch_shapes=[pltpu.VMEM(whitened.shape, jnp.float32) for _ in range(2)]
        + [pltpu.VMEM((8, times), jnp.float32), pltpu.VMEM((lines, 3 * lines), jnp.bfloat16)]
        + [pltpu.VMEM((3 * times, times), jnp.bfloat16) for _ in range(2)]
        + [pltpu.VMEM((rows, times), jnp.float32)]
        + [ring(jnp.float32) for _ in range(3)]
        + [ring(jnp.int32) for _ in range(2)]
        + [ring(jnp.float32) for _ in range(4)]
        + [pltpu.VMEM((RING // parts, rows, times), jnp.float32)]
        + [stacked() for _ in range(2)]
        + [
            pltpu.VMEM((rows, LANES), jnp.float32),
            pltpu.VMEM((group, 8, LANES), jnp.float32),
            pltpu.VMEM((QUARTERS, 8, LANES), jnp.float32),
        ]
        + [dma((3,))]
        + [dma((RING,)) for _ in range(8)]
        + [dma] * 7,
        compiler_params=pltpu.CompilerParams(
            collective_id=0, has_side_effects=True, vmem_limit_bytes=VMEM_BYTES
        ),
    )(whitened, counts, exposure, east, north, time)


def finish_kernel(scale, h_ref, w_ref, north, terms, out_ref, density, left):
    @pl.when(pl.program_id(0) == 0)
    def _():
        left[...] = hhl(north[...].T, 1)
        density[0] = jnp.sum(terms[...]) * scale

    for a in range(h_ref.shape[0]):
        adjoint = dot(left[...], hlh(h_ref[a], 0))
        out_ref[a] = field_scale * adjoint - w_ref[a]


def finish(partly, whitened, north, terms, scale):
    planes, lines, times = whitened.shape
    block = min(planes, 8)
    some = pl.BlockSpec((block, lines, times), lambda i: (i, 0, 0))
    fixed = lambda array: pl.BlockSpec(array.shape, lambda i: (0, 0))
    return pl.pallas_call(
        functools.partial(finish_kernel, scale),
        grid=(planes // block,),
        out_shape=[jax.ShapeDtypeStruct(whitened.shape, jnp.float32), jax.ShapeDtypeStruct((1,), jnp.float32)],
        in_specs=[some] * 2 + [fixed(north), fixed(terms)],
        out_specs=[some, pl.BlockSpec(memory_space=pltpu.SMEM)],
        scratch_shapes=[pltpu.VMEM((lines, 3 * lines), jnp.bfloat16)],
    )(partly, whitened, north, terms)


def per_device(whitened, counts, exposure, cholesky_east, cholesky_north, cholesky_time):
    slabs = lax.axis_size("slab")
    cell_count = whitened.shape[0] * whitened.shape[1] * whitened.shape[2] * slabs
    partly, terms = exchange(
        whitened, counts, exposure, cholesky_east, cholesky_north, cholesky_time, slabs // QUARTERS
    )
    gradient, density = finish(partly, whitened, cholesky_north, terms, 1.0 / cell_count)
    return (gradient, density)


def solution(mesh):
    placed = (
        P(("chain", "slab"), None, None),
        P(("chain", "slab"), None, None),
        P(("chain", "slab"), None, None),
        P(),
        P(),
        P(),
    )
    return jax.shard_map(
        per_device,
        mesh=mesh,
        in_specs=placed,
        out_specs=(P(("chain", "slab"), None, None), P("chain")),
        check_vma=False,
    )
```

time: 473 us -> 409 us (0.86)
  Pallas kernels: 471 us -> 408 us
    pallas_call x1, Pallas kernels: 429 us -> 397 us  [exchange(): pl.pallas_call(functools.partial(kernel, group, parts), out_shape=(jax.Sh...]
    pallas_call x2 -> x1, Pallas kernels: 41.9 us -> 10.7 us  [finish(): pl.pallas_call(functools.partial(finish_kernel, scale), grid=(planes // b...]
where the time goes in v1:
time: 409 us
  Pallas kernels  408 us (100%)
    pallas_call x1, Pallas kernels, exchange(): pl.pallas_call(functools.partial(kernel, group, parts), out_shape=(jax.Sh...  397 us
    pallas_call x1, Pallas kernels, finish(): pl.pallas_call(functools.partial(finish_kernel, scale), grid=(planes // b...  10.7 us

profile of v1, /device:TPU:0, one launch (start us, length us, event | category | flops | bytes accessed | tf_op | source)
XLA Modules:
  0.0 408.7 jit_solution(2809267527699034530)
XLA Ops:
  0.6 397.3 %shard_map.77 = (f32[32,256,256]{2,1,0:T(8,128)}, f32[8,128]{1,0:T(8,128)}) custom-call(f32[32,256,256]{2,1,0:T(8,128)} %w_ref.1, s32[32,256,256]{2,1,0:T(8,128)} %cnt_hbm.1, s32[32,256,256]{2,1,0:T(8,128)} %exp_hbm.1, f32[512,512]{1,0:T(8,128)} %east.1, f32[256,256]{1,0:T(8,128)} %north.3, f32[256,256]{1,0:T(8,128)} %time.1), custom_call_target="tpu_custom_call" | custom-call | tf_op jit(solution)/shard_map/pallas_call | solution.py:373
  398.0 10.7 %shard_map.78 = (f32[32,256,256]{2,1,0:T(8,128)}, f32[1]{0:T(128)}) custom-call(f32[32,256,256]{2,1,0:T(8,128)} %get-tuple-element.4.h_ref, f32[32,256,256]{2,1,0:T(8,128)} %w_ref.1, f32[256,256]{1,0:T(8,128)} %north.3, f32[8,128]{1,0:T(8,128)} %get-tuple-element.5.terms), custom_call_target="tpu_custom_call" | custom-call | tf_op jit(solution)/shard_map/pallas_call | solution.py:420

commit v2 on v1

--- a/solution.py
+++ b/solution.py
@@ -11,11 +11,12 @@
 QUARTERS = 4
 LANES = 128
 AHEAD = 4
+EARLY = 3
 RING = 16
 BANDS = 4
 SENT = 4
-FORWARD_LAG = (2, 4, 0, 0)
-BACKWARD_LAG = (10, 8, 4, 1)
+FORWARD_LAG = (2, 4, 1, 0)
+BACKWARD_LAG = (10, 9, 6, 4)
 VMEM_BYTES = 67043328
 
 
@@ -276,17 +277,19 @@
 
     ahead = min(AHEAD, chunks)
 
-    def start(arrays):
+    def start(lower, upper, arrays):
         def body(chunk, carry):
             spread(chunk, arrays)
             return carry
 
-        lax.fori_loop(0, ahead, body, 0)
-
-    start((1, 2))
+        lax.fori_loop(lower, upper, body, 0)
+
+    early = min(EARLY, ahead)
+    start(0, early, (1, 2))
     await_bytes(held.at[first], load_first)
     begin()
-    start((0,))
+    start(0, early, (0,))
+    start(early, ahead, (0, 1, 2))
     await_bytes(held.at[rest], load_rest)
     last = chunks + max(FORWARD_LAG)
 
@@ -414,7 +417,7 @@
 
 def finish(partly, whitened, north, terms, scale):
     planes, lines, times = whitened.shape
-    block = min(planes, 8)
+    block = min(planes, 16)
     some = pl.BlockSpec((block, lines, times), lambda i: (i, 0, 0))
     fixed = lambda array: pl.BlockSpec(array.shape, lambda i: (0, 0))
     return pl.pallas_call(

time: 409 us -> 402 us (0.983)
  Pallas kernels: 408 us -> 401 us
    pallas_call x1, Pallas kernels: 397 us -> 391 us  [exchange(): pl.pallas_call(functools.partial(kernel, group, parts), out_shape=(jax.Sh...]
where the time goes in v2:
time: 402 us
  Pallas kernels  401 us (100%)
    pallas_call x1, Pallas kernels, exchange(): pl.pallas_call(functools.partial(kernel, group, parts), out_shape=(jax.Sh...  391 us
    pallas_call x1, Pallas kernels, finish(): pl.pallas_call(functools.partial(finish_kernel, scale), grid=(planes // b...  9.81 us

profile of v2, /device:TPU:0, one launch (start us, length us, event | category | flops | bytes accessed | tf_op | source)
XLA Modules:
  0.0 401.9 jit_solution(5470954314143199356)
XLA Ops:
  0.6 391.5 %shard_map.77 = (f32[32,256,256]{2,1,0:T(8,128)}, f32[8,128]{1,0:T(8,128)}) custom-call(f32[32,256,256]{2,1,0:T(8,128)} %w_ref.1, s32[32,256,256]{2,1,0:T(8,128)} %cnt_hbm.1, s32[32,256,256]{2,1,0:T(8,128)} %exp_hbm.1, f32[512,512]{1,0:T(8,128)} %east.1, f32[256,256]{1,0:T(8,128)} %north.3, f32[256,256]{1,0:T(8,128)} %time.1), custom_call_target="tpu_custom_call" | custom-call | tf_op jit(solution)/shard_map/pallas_call | solution.py:376
  392.1 9.8 %shard_map.78 = (f32[32,256,256]{2,1,0:T(8,128)}, f32[1]{0:T(128)}) custom-call(f32[32,256,256]{2,1,0:T(8,128)} %get-tuple-element.4.h_ref, f32[32,256,256]{2,1,0:T(8,128)} %w_ref.1, f32[256,256]{1,0:T(8,128)} %north.3, f32[8,128]{1,0:T(8,128)} %get-tuple-element.5.terms), custom_call_target="tpu_custom_call" | custom-call | tf_op jit(solution)/shard_map/pallas_call | solution.py:423

commit v3 on v2

--- a/solution.py
+++ b/solution.py
@@ -10,13 +10,13 @@
 field_scale = 0.6
 QUARTERS = 4
 LANES = 128
-AHEAD = 4
+AHEAD = 3
 EARLY = 3
-RING = 16
+RING = 12
 BANDS = 4
 SENT = 4
 FORWARD_LAG = (2, 4, 1, 0)
-BACKWARD_LAG = (10, 9, 6, 4)
+BACKWARD_LAG = (9, 8, 6, 4)
 VMEM_BYTES = 67043328
 
 
@@ -41,10 +41,10 @@
 
 
 def kernel(
-    group, parts, w_hbm, cnt_hbm, exp_hbm, east, north, time, out_hbm, density,
+    group, parts, w_hbm, cnt_hbm, exp_hbm, east_hbm, north, time, out_hbm, density,
     held, q_own, squares, left, onto, back, pending, own, f0, f1, cnt, wgt, b0, b1, res, spare, out, fwd, bwd, acc, near, far,
     send_in, recv_p, recv_o, recv_f, recv_b, send_z, send_r, send_g, keep_g, recv_g,
-    send_near, recv_near, send_far, recv_far, load_first, load_rest,
+    send_near, recv_near, send_far, recv_far, load_first, load_rest, load_east, east,
 ):
     slab = lax.axis_index("slab")
     quarter = slab // group
@@ -63,6 +63,7 @@
     rest = (slice(None), pl.ds(band, north_cells - band))
     pltpu.make_async_copy(w_hbm.at[first], held.at[first], load_first).start()
     pltpu.make_async_copy(w_hbm.at[rest], held.at[rest], load_rest).start()
+    pltpu.make_async_copy(east_hbm, east, load_east).start()
 
     def device(quarter_of, place_of):
         return {"slab": quarter_of * group + place_of}
@@ -291,6 +292,7 @@
     start(0, early, (0,))
     start(early, ahead, (0, 1, 2))
     await_bytes(held.at[rest], load_rest)
+    await_bytes(east, load_east)
     last = chunks + max(FORWARD_LAG)
 
     for q in range(QUARTERS):
@@ -379,7 +381,7 @@
             jax.ShapeDtypeStruct(whitened.shape, jnp.float32),
             jax.ShapeDtypeStruct((8, LANES), jnp.float32),
         ),
-        in_specs=[any_space] * 3 + [in_vmem] * 3,
+        in_specs=[any_space] * 4 + [in_vmem] * 2,
         out_specs=(any_space, in_vmem),
         scratch_shapes=[pltpu.VMEM(whitened.shape, jnp.float32) for _ in range(2)]
         + [pltpu.VMEM((8, times), jnp.float32), pltpu.VMEM((lines, 3 * lines), jnp.bfloat16)]
@@ -397,7 +399,8 @@
         ]
         + [dma((3,))]
         + [dma((RING,)) for _ in range(8)]
-        + [dma] * 7,
+        + [dma] * 8
+        + [pltpu.VMEM(east.shape, jnp.float32)],
         compiler_params=pltpu.CompilerParams(
             collective_id=0, has_side_effects=True, vmem_limit_bytes=VMEM_BYTES
         ),

time: 402 us -> 401 us (level)
  no operation moved by 1% of the time
where the time goes in v3:
time: 401 us
  Pallas kernels  401 us (100%)
    pallas_call x1, Pallas kernels, exchange(): pl.pallas_call(functools.partial(kernel, group, parts), out_shape=(jax.Sh...  391 us
    pallas_call x1, Pallas kernels, finish(): pl.pallas_call(functools.partial(finish_kernel, scale), grid=(planes // b...  9.81 us

profile of v3, /device:TPU:0, one launch (start us, length us, event | category | flops | bytes accessed | tf_op | source)
XLA Modules:
  0.0 401.3 jit_solution(5762259274218232226)
XLA Ops:
  0.6 390.9 %shard_map.77 = (f32[32,256,256]{2,1,0:T(8,128)}, f32[8,128]{1,0:T(8,128)}) custom-call(f32[32,256,256]{2,1,0:T(8,128)} %w_ref.1, s32[32,256,256]{2,1,0:T(8,128)} %cnt_hbm.1, s32[32,256,256]{2,1,0:T(8,128)} %exp_hbm.1, f32[512,512]{1,0:T(8,128)} %east_hbm.1, f32[256,256]{1,0:T(8,128)} %north.3, f32[256,256]{1,0:T(8,128)} %time.1), custom_call_target="tpu_custom_call" | custom-call | tf_op jit(solution)/shard_map/pallas_call | solution.py:378
  391.5 9.8 %shard_map.78 = (f32[32,256,256]{2,1,0:T(8,128)}, f32[1]{0:T(128)}) custom-call(f32[32,256,256]{2,1,0:T(8,128)} %get-tuple-element.4.h_ref, f32[32,256,256]{2,1,0:T(8,128)} %w_ref.1, f32[256,256]{1,0:T(8,128)} %north.3, f32[8,128]{1,0:T(8,128)} %get-tuple-element.5.terms), custom_call_target="tpu_custom_call" | custom-call | tf_op jit(solution)/shard_map/pallas_call | solution.py:426
